TPU v7x, 32 devices: a whole 2x2x4 slice. The times are simulated.
32 devices in a mesh: batch: 8 (over z, y), tensor: 4 (over x, core).
Axes of the slice: x: 2, y: 2, z: 4, core: 2. Of those that a mesh axis runs over, the one named last changes fastest.
Arguments:
- tokens: bfloat16 [12288, 768], P('batch'), may hold values from -6 to 6
- lengths: int32 [8], P('batch'), may hold values from 1024 to 1536, as said below
- w_query: bfloat16 [768, 768], P('batch', 'tensor'), may hold values from -0.4375 to 0.4375
- w_key: bfloat16 [768, 768], P('batch', 'tensor'), may hold values from -0.21875 to 0.21875
- w_value: bfloat16 [768, 768], P('batch', 'tensor'), may hold values from -0.21875 to 0.21875
- w_out: bfloat16 [768, 768], P('tensor', 'batch'), may hold values from -0.875 to 0.875
- w_up: bfloat16 [768, 3072], P('batch', 'tensor'), may hold values from -0.21875 to 0.21875
- w_down: bfloat16 [3072, 768], P('tensor', 'batch'), may hold values from -0.109375 to 0.109375
- norm_gain: bfloat16 [2, 768], P(None, 'batch'), may hold values from 0.099609375 to 1.8984375
- norm_shift: bfloat16 [2, 768], P(None, 'batch'), may hold values from -3 to 3
- out_grad: bfloat16 [12288, 768], P('batch'), may hold values from -6 to 6
Outputs:
- layer_out: bfloat16 [12288, 768], P('batch')
- grad_input: bfloat16 [12288, 768], P('batch')
- grad_query: float32 [768, 768], P('batch', 'tensor')
- grad_key: float32 [768, 768], P('batch', 'tensor')
- grad_value: float32 [768, 768], P('batch', 'tensor')
- grad_out: float32 [768, 768], P('tensor', 'batch')
- grad_up: float32 [768, 3072], P('batch', 'tensor')
- grad_down: float32 [3072, 768], P('tensor', 'batch')
- grad_gain: float32 [2, 768], P(None, 'batch')
- grad_shift: float32 [2, 768], P(None, 'batch')
Inputs may be any that keep to these rules, and one draw needn't show every extreme that they name: `lengths`: each sequence's valid tokens; some sequence fills all 1536 slots.
All inputs are finite; a program needn't handle non-finite values.
Results may differ from a plain program's by a relative error of at most 0.017.
Values may be sent and summed in bfloat16 or wider, within the bound.
No kernel may reach another device: no remote copies, remote signals or barrier semaphores. Data moves between devices by JAX's collectives and lax.ppermute only.
A program may use at most 192 MiB of HBM per device.

v0:
```python
import jax
import jax.numpy as jnp
from jax import lax
from jax.sharding import PartitionSpec as P

HD = 64
epsilon = 1e-05


def cut_along(value, dim, length):
    shape = value.shape
    parts = value.reshape(*shape[:dim], length, shape[dim] // length, *shape[dim + 1 :])
    return jnp.moveaxis(parts, dim, 0)


def summed_on_arrival(value, axis, dim):
    length = lax.axis_size(axis)
    parts = lax.all_to_all(cut_along(value, dim, length), axis, 0, 0, tiled=True)
    return jnp.sum(parts.astype(jnp.float32), axis=0)


def normalize_keep(values, gain_row, shift_row):
    middle = jnp.mean(values, axis=-1, keepdims=True)
    centred = values - middle
    spread = jnp.mean(centred * centred, axis=-1, keepdims=True)
    inverse = lax.rsqrt(spread + epsilon)
    scaled = centred * inverse
    return (scaled * gain_row + shift_row, scaled, inverse)


def normalize_back(grad_normed, scaled, inverse, gain_row):
    grad_scaled = grad_normed * gain_row
    mean_grad = jnp.mean(grad_scaled, axis=-1, keepdims=True)
    mean_cross = jnp.mean(grad_scaled * scaled, axis=-1, keepdims=True)
    grad_values = inverse * (grad_scaled - mean_grad - scaled * mean_cross)
    return (grad_values, jnp.sum(grad_normed * scaled, axis=0), jnp.sum(grad_normed, axis=0))


def multiply(left_mat, right_mat):
    return jnp.dot(left_mat, right_mat, preferred_element_type=jnp.float32)


def inner_rows(left_mat, right_mat):
    return lax.dot_general(
        left_mat, right_mat, (((0,), (0,)), ((), ())), preferred_element_type=jnp.float32
    )


def outer_cols(left_mat, right_mat):
    return lax.dot_general(
        left_mat, right_mat, (((1,), (1,)), ((), ())), preferred_element_type=jnp.float32
    )


def gelu_tanh(values):
    return jax.nn.gelu(values, approximate=True)


def score_block(queries_blk, keys_part, row_pos, key_pos, length, scaling):
    raw_scores = jnp.einsum(
        "qhd,khd->hqk", queries_blk, keys_part, preferred_element_type=jnp.float32
    )
    scores = raw_scores * scaling
    allowed = (key_pos[None, :] <= row_pos[:, None]) & (key_pos[None, :] < length)
    magnitude = jnp.where(allowed[None], jnp.abs(scores), -1e30)
    return (scores, magnitude)


def attend_forward(queries, key_rows, value_rows, length, block_rows, scaling):
    seq_rows = queries.shape[0]
    position = jnp.arange(seq_rows, dtype=jnp.int32)
    outputs = []
    log_sums = []
    for number in range(seq_rows // block_rows):
        begin_row = number * block_rows
        end_row = begin_row + block_rows
        scores, magnitude = score_block(
            queries[begin_row:end_row],
            key_rows[:end_row],
            position[begin_row:end_row],
            position[:end_row],
            length,
            scaling,
        )
        row_max = jnp.max(magnitude, axis=-1, keepdims=True)
        exponent = jnp.exp(magnitude - row_max)
        row_sum = jnp.sum(exponent, axis=-1, keepdims=True)
        weights = (jnp.sign(scores) * (exponent / row_sum)).astype(jnp.bfloat16)
        outputs.append(
            jnp.einsum(
                "hqk,khd->qhd", weights, value_rows[:end_row], preferred_element_type=jnp.float32
            )
        )
        log_sums.append(row_max + jnp.log(row_sum))
    return (jnp.concatenate(outputs, axis=0), jnp.concatenate(log_sums, axis=1))


def attend_back(queries, key_rows, value_rows, grad_mixed, log_sums, length, block_rows, scaling):
    seq_rows = queries.shape[0]
    position = jnp.arange(seq_rows, dtype=jnp.int32)
    grad_queries = []
    grad_keys = jnp.zeros(key_rows.shape, jnp.float32)
    grad_values = jnp.zeros(value_rows.shape, jnp.float32)
    for number in range(seq_rows // block_rows):
        begin_row = number * block_rows
        end_row = begin_row + block_rows
        scores, magnitude = score_block(
            queries[begin_row:end_row],
            key_rows[:end_row],
            position[begin_row:end_row],
            position[:end_row],
            length,
            scaling,
        )
        probability = jnp.exp(magnitude - log_sums[:, begin_row:end_row])
        signs = jnp.sign(scores)
        weights = signs * probability
        grad_blk = grad_mixed[begin_row:end_row]
        grad_weights = jnp.einsum(
            "qhd,khd->hqk", grad_blk, value_rows[:end_row], preferred_element_type=jnp.float32
        )
        delta_row = jnp.sum(weights * grad_weights, axis=-1, keepdims=True)
        grad_raw = (signs * probability * (signs * grad_weights - delta_row) * scaling).astype(
            jnp.bfloat16
        )
        grad_queries.append(
            jnp.einsum(
                "hqk,khd->qhd", grad_raw, key_rows[:end_row], preferred_element_type=jnp.float32
            )
        )
        grad_keys = grad_keys.at[:end_row].add(
            jnp.einsum(
                "hqk,qhd->khd",
                grad_raw,
                queries[begin_row:end_row],
                preferred_element_type=jnp.float32,
            )
        )
        grad_values = grad_values.at[:end_row].add(
            jnp.einsum(
                "hqk,qhd->khd",
                weights.astype(jnp.bfloat16),
                grad_blk,
                preferred_element_type=jnp.float32,
            )
        )
    return (jnp.concatenate(grad_queries, axis=0), grad_keys, grad_values)


def per_device(
    tokens, lengths, w_query, w_key, w_value, w_out, w_up, w_down, norm_gain, norm_shift, out_grad
):
    seq_rows = tokens.shape[0]
    seq_count = lengths.shape[0]
    seq_len = seq_rows // seq_count
    position = jnp.arange(seq_rows, dtype=jnp.int32)
    slot_length = jnp.repeat(lengths, seq_len)
    is_valid = (position % seq_len < slot_length).astype(jnp.float32)[:, None]
    block_rows = min(512, seq_len)
    scaling = float(HD) ** (-0.5)
    gathered = (
        lax.all_gather(w_query, "batch", axis=0, tiled=True),
        lax.all_gather(w_key, "batch", axis=0, tiled=True),
        lax.all_gather(w_value, "batch", axis=0, tiled=True),
        lax.all_gather(w_out, "batch", axis=1, tiled=True),
        lax.all_gather(w_up, "batch", axis=0, tiled=True),
        lax.all_gather(w_down, "batch", axis=1, tiled=True),
        lax.all_gather(norm_gain, "batch", axis=1, tiled=True),
        lax.all_gather(norm_shift, "batch", axis=1, tiled=True),
    )
    full_query, full_key, full_value, full_out, full_up, full_down, gain_full, shift_full = gathered
    gain_rows = gain_full.astype(jnp.float32)
    shift_rows = shift_full.astype(jnp.float32)
    head_count = full_query.shape[1] // HD

    def per_sequence(values):
        return values.reshape(seq_count, seq_len, head_count, HD)

    inputs = tokens.astype(jnp.float32)
    normed, scaled_one, inverse_one = normalize_keep(inputs, gain_rows[0], shift_rows[0])
    normed_low = normed.astype(jnp.bfloat16)
    queries = (
        multiply(normed_low, full_query).astype(jnp.bfloat16).reshape(seq_rows, head_count, HD)
    )
    key_rows = multiply(normed_low, full_key).astype(jnp.bfloat16).reshape(seq_rows, head_count, HD)
    value_rows = (
        multiply(normed_low, full_value).astype(jnp.bfloat16).reshape(seq_rows, head_count, HD)
    )

    def forward_one(items):
        return attend_forward(items[0], items[1], items[2], items[3], block_rows, scaling)

    mixed_heads, log_sums = lax.map(
        forward_one,
        (per_sequence(queries), per_sequence(key_rows), per_sequence(value_rows), lengths),
    )
    mixed_low = mixed_heads.reshape(seq_rows, head_count * HD).astype(jnp.bfloat16)
    attn_partial = multiply(mixed_low, full_out)
    hidden = inputs + lax.psum(attn_partial, "tensor")
    normed_two, scaled_two, inverse_two = normalize_keep(hidden, gain_rows[1], shift_rows[1])
    normed_two_low = normed_two.astype(jnp.bfloat16)
    up_proj = multiply(normed_two_low, full_up)
    active_full, gelu_pull = jax.vjp(gelu_tanh, up_proj)
    active = active_full.astype(jnp.bfloat16)
    down_partial = multiply(active, full_down)
    branch = lax.psum(down_partial.astype(jnp.bfloat16), "tensor").astype(jnp.float32)
    out_rows = ((hidden + branch) * is_valid).astype(jnp.bfloat16)
    grad_rows = out_grad * is_valid.astype(jnp.bfloat16)
    grad_down = inner_rows(active, grad_rows)
    grad_active = outer_cols(grad_rows, full_down)
    grad_upper = gelu_pull(grad_active)[0].astype(jnp.bfloat16)
    grad_up = inner_rows(normed_two_low, grad_upper)
    mid_partial = outer_cols(grad_upper, full_up)
    grad_normed_two = lax.psum(mid_partial, "tensor")
    grad_from_two, gain_two, shift_two = normalize_back(
        grad_normed_two, scaled_two, inverse_two, gain_rows[1]
    )
    grad_hidden = grad_rows.astype(jnp.float32) + grad_from_two
    grad_attn = grad_hidden.astype(jnp.bfloat16)
    grad_out = inner_rows(mixed_low, grad_attn)
    grad_mixed = (
        outer_cols(grad_attn, full_out).astype(jnp.bfloat16).reshape(seq_rows, head_count, HD)
    )

    def backward_one(items):
        return attend_back(
            items[0], items[1], items[2], items[3], items[4], items[5], block_rows, scaling
        )

    grad_queries, grad_keys, grad_values = lax.map(
        backward_one,
        (
            per_sequence(queries),
            per_sequence(key_rows),
            per_sequence(value_rows),
            per_sequence(grad_mixed),
            log_sums,
            lengths,
        ),
    )
    queries_low = grad_queries.astype(jnp.bfloat16).reshape(seq_rows, head_count * HD)
    keys_low = grad_keys.astype(jnp.bfloat16).reshape(seq_rows, head_count * HD)
    values_low = grad_values.astype(jnp.bfloat16).reshape(seq_rows, head_count * HD)
    grad_query = inner_rows(normed_low, queries_low)
    grad_key = inner_rows(normed_low, keys_low)
    grad_value = inner_rows(normed_low, values_low)
    partial_in = (
        outer_cols(queries_low, full_query)
        + outer_cols(keys_low, full_key)
        + outer_cols(values_low, full_value)
    )
    grad_normed = lax.psum(partial_in.astype(jnp.bfloat16), "tensor").astype(jnp.float32)
    grad_from_one, gain_one, shift_one = normalize_back(
        grad_normed, scaled_one, inverse_one, gain_rows[0]
    )
    grad_input = (grad_hidden + grad_from_one).astype(jnp.bfloat16)
    gain_pair = jnp.stack([gain_one, gain_two])
    shift_pair = jnp.stack([shift_one, shift_two])
    everything = (
        summed_on_arrival(grad_query.astype(jnp.bfloat16), "batch", 0),
        summed_on_arrival(grad_key.astype(jnp.bfloat16), "batch", 0),
        summed_on_arrival(grad_value.astype(jnp.bfloat16), "batch", 0),
        summed_on_arrival(grad_out.astype(jnp.bfloat16), "batch", 1),
        summed_on_arrival(grad_up.astype(jnp.bfloat16), "batch", 0),
        summed_on_arrival(grad_down.astype(jnp.bfloat16), "batch", 1),
        summed_on_arrival(gain_pair.astype(jnp.bfloat16), "batch", 1),
        summed_on_arrival(shift_pair.astype(jnp.bfloat16), "batch", 1),
    )
    (
        shard_query,
        shard_key,
        shard_value,
        shard_out,
        shard_up,
        shard_down,
        shard_gain,
        shard_shift,
    ) = everything
    return (
        out_rows,
        grad_input,
        shard_query,
        shard_key,
        shard_value,
        shard_out,
        shard_up,
        shard_down,
        shard_gain,
        shard_shift,
    )


def solution(mesh):
    in_specs = (
        P("batch", None),
        P("batch"),
        P("batch", "tensor"),
        P("batch", "tensor"),
        P("batch", "tensor"),
        P("tensor", "batch"),
        P("batch", "tensor"),
        P("tensor", "batch"),
        P(None, "batch"),
        P(None, "batch"),
        P("batch", None),
    )
    out_specs = (
        P("batch", None),
        P("batch", None),
        P("batch", "tensor"),
        P("batch", "tensor"),
        P("batch", "tensor"),
        P("tensor", "batch"),
        P("batch", "tensor"),
        P("tensor", "batch"),
        P(None, "batch"),
        P(None, "batch"),
    )
    return jax.shard_map(
        per_device, mesh=mesh, in_specs=in_specs, out_specs=out_specs, check_vma=False
    )
```

profile of v0, /device:TPU:0, one launch (start us, length us, event | category | flops | bytes accessed | tf_op | source)
XLA Modules:
  0.0 746.9 jit_solution(5650384383720290563)
XLA Ops:
  9.3 22.3 %all-gather = bf16[8,96,2]{1,2,0:T(2,128)(2,1)S(1)} all-gather(bf16[1,96,2]{1,2,0:T(2,128)(2,1)} %bitcast.189), channel_id=1, replica_groups=mesh['batch'=8,'tensor'=4] {'batch'}, dimensions={0}, use_global_device_ids=true | all-gather | bytes 3456 | tf_op jit(solution)/shard_map/all_gather | solution.py:168
  32.3 16.4 %all-gather.1 = bf16[8,96,2]{1,2,0:T(2,128)(2,1)S(1)} all-gather(bf16[1,96,2]{1,2,0:T(2,128)(2,1)} %bitcast.190), channel_id=1, replica_groups=mesh['batch'=8,'tensor'=4] {'batch'}, dimensions={0}, use_global_device_ids=true | all-gather | bytes 3456 | tf_op jit(solution)/shard_map/all_gather | solution.py:169
  54.0 31.0 %all_gather.28 = bf16[768,192]{1,0:T(8,128)(2,1)S(1)} all-gather(bf16[96,192]{1,0:T(8,128)(2,1)S(1)} %copy-done.50), channel_id=1, replica_groups=mesh['batch'=8,'tensor'=4] {'batch'}, dimensions={0}, use_global_device_ids=true | all-gather | bytes 331776 | tf_op jit(solution)/shard_map/all_gather | solution.py:163
  88.7 31.2 %all_gather.26 = bf16[768,192]{1,0:T(8,128)(2,1)S(1)} all-gather(bf16[96,192]{1,0:T(8,128)(2,1)S(1)} %copy-done.51), channel_id=1, replica_groups=mesh['batch'=8,'tensor'=4] {'batch'}, dimensions={0}, use_global_device_ids=true | all-gather | bytes 331776 | tf_op jit(solution)/shard_map/all_gather | solution.py:164
  125.1 31.3 %all_gather.29 = bf16[192,768]{0,1:T(8,128)(2,1)S(1)} all-gather(bf16[192,96]{0,1:T(8,128)(2,1)} %copy.70), channel_id=1, replica_groups=mesh['batch'=8,'tensor'=4] {'batch'}, dimensions={1}, use_global_device_ids=true | all-gather | bytes 331776 | tf_op jit(solution)/shard_map/all_gather | solution.py:165
  156.4 31.2 %all_gather.27 = bf16[768,192]{1,0:T(8,128)(2,1)S(1)} all-gather(bf16[96,192]{1,0:T(8,128)(2,1)} %param.29), channel_id=1, replica_groups=mesh['batch'=8,'tensor'=4] {'batch'}, dimensions={0}, use_global_device_ids=true | all-gather | bytes 331776 | tf_op jit(solution)/shard_map/all_gather | solution.py:162
  210.0 6.4 fusion.150
  222.0 90.3 %all-reduce.7.cloned.1.call-done = f32[1536,768]{1,0:T(8,128)} async-done(((f32[1536,768]{1,0:T(8,128)}), f32[1536,768]{1,0:T(8,128)}) %all-reduce.7.cloned.1.call-update) | async-done | bytes 4718608 | tf_op jit(solution)/shard_map/psum | solution.py:199
  319.5 6.2 fusion.203
  325.7 7.0 fusion.31
  341.1 6.8 fusion.107
  347.9 5.9 all-to-all-start.5
  353.8 5.6 convolution_convert_fusion.5
  359.4 6.8 convolution_convert_fusion
  366.1 66.6 %all-reduce.9.cloned.1.call-done = f32[1536,768]{1,0:T(8,128)} async-done(((f32[1536,768]{1,0:T(8,128)}), f32[1536,768]{1,0:T(8,128)}) %all-reduce.9.cloned.1.call-update) | async-done | bytes 4718608 | tf_op jit(solution)/shard_map/psum | solution.py:214
  432.7 5.6 multiply_reduce_fusion.2
  450.4 9.7 %fusion.128 = f32[512,3,64]{0,2,1:T(8,128)} fusion(bf16[512,3,64]{0,2,1:T(8,128)(2,1)} %bitcast.178, f32[3,512,512]{1,2,0:T(8,128)} %fusion.205, f32[3,512,512]{1,2,0:T(8,128)} %copy-done.18, f32[3,512]{1,0:T(4,128)S(1)} %copy-done.61, pred[512,512]{0,1:T(8,128)(4,1)} %copy-done.28), kind=kOutput, calls=%fused_computation.130 | convolution fusion | flops 114821120 | bytes 7149568 | tf_op jit(solution)/shard_map/while/body/eval_jaxpr/hqk,qhd->khd/dot_general | solution.py:132
  465.0 5.1 fusion.207
  470.0 20.1 %fusion.145 = bf16[3,64,512]{2,1,0:T(8,128)(2,1)} fusion(bf16[1024,3,64]{0,2,1:T(8,128)(2,1)} %bitcast.171, f32[3,512,1024]{2,1,0:T(8,128)} %fusion.206, f32[3,512,1024]{2,1,0:T(8,128)} %copy-done.7, f32[3,512]{1,0:T(4,128)} %log_add_fusion.1, pred[512,1024]{1,0:T(8,128)(4,1)} %copy-done.23), kind=kOutput, calls=%fused_computation.139 | convolution fusion | flops 229739008 | bytes 13703168 | tf_op jit(solution)/shard_map/while/body/eval_jaxpr/hqk,khd->qhd/dot_general | solution.py:127
  493.5 9.8 %fusion.141 = bf16[3,64,512]{2,1,0:T(8,128)(2,1)} fusion(bf16[512,3,64]{0,2,1:T(8,128)(2,1)} %bitcast.179, f32[3,512,512]{1,2,0:T(8,128)} %fusion.205, f32[3,512,512]{1,2,0:T(8,128)} %copy-done.18, f32[3,512]{1,0:T(4,128)S(1)} %copy-done.61, pred[512,512]{0,1:T(8,128)(4,1)} %copy-done.28), kind=kOutput, calls=%fused_computation.137 | convolution fusion | flops 114919424 | bytes 6952960 | tf_op jit(solution)/shard_map/while/body/eval_jaxpr/hqk,khd->qhd/dot_general | solution.py:127
  503.3 26.8 %fusion.138 = bf16[3,64,512]{2,1,0:T(8,128)(2,1)} fusion(bf16[1536,3,64]{0,2,1:T(8,128)(2,1)S(1)} %bitcast.154, f32[3,512,1536]{2,1,0:T(8,128)} %fusion.207, f32[3,512,1536]{2,1,0:T(8,128)} %copy-done.6, f32[3,512]{1,0:T(4,128)S(1)} %copy-done.62, pred[512,1536]{1,0:T(8,128)(4,1)} %copy-done.16), kind=kOutput, calls=%fused_computation.136 | convolution fusion | flops 344558592 | bytes 20453376 | tf_op jit(solution)/shard_map/while/body/eval_jaxpr/hqk,khd->qhd/dot_general | solution.py:127
  530.0 20.4 %fusion.119 = f32[1536,3,64]{0,2,1:T(8,128)} fusion(f32[1536,3,64]{0,2,1:T(8,128)} %scatter-add.14, bf16[512,3,64]{0,2,1:T(8,128)(2,1)} %bitcast.176, f32[3,512,1024]{2,1,0:T(8,128)} %fusion.206, f32[3,512,1024]{2,1,0:T(8,128)} %copy-done.7, f32[3,512]{1,0:T(4,128)S(1)} %copy-done.63, pred[512,1024]{1,0:T(8,128)(4,1)} %copy-done.23), kind=kOutput, calls=%fused_computation.123 | convolution fusion | flops 229837312 | bytes 28000256 | tf_op jit(solution)/shard_map/while/body/eval_jaxpr/hqk,qhd->khd/dot_general | solution.py:132
  550.5 27.8 %fusion.76 = bf16[1536,3,64]{0,2,1:T(8,128)(2,1)} fusion(f32[1536,3,64]{0,2,1:T(8,128)} %fusion.119, bf16[512,3,64]{0,2,1:T(8,128)(2,1)S(1)} %bitcast.174, f32[3,512,1536]{2,1,0:T(8,128)} %fusion.207, f32[3,512,1536]{2,1,0:T(8,128)} %copy-done.6, f32[3,512]{1,0:T(4,128)S(1)} %copy-done.62, pred[512,1536]{1,0:T(8,128)(4,1)} %copy-done.16), kind=kOutput, calls=%fused_computation.94 | convolution fusion | flops 345050112 | bytes 21633024 | tf_op jit(solution)/shard_map/while/body/eval_jaxpr/hqk,qhd->khd/dot_general | solution.py:132
  582.4 7.9 %fusion.125 = f32[1536,3,64]{0,2,1:T(8,128)} fusion(f32[1536,3,64]{0,2,1:T(8,128)} %scatter-add.16, bf16[512,3,64]{0,2,1:T(8,128)(2,1)S(1)} %bitcast.166, f32[3,512]{1,0:T(4,128)S(1)} %copy-done.63, pred[512,1024]{1,0:T(8,128)(4,1)S(1)} %copy-done.24, f32[3,512,1024]{2,1,0:T(8,128)} %copy-done.7), kind=kOutput, calls=%fused_computation.125 | convolution fusion | flops 212533248 | bytes 8591360 | tf_op jit(solution)/shard_map/while/body/eval_jaxpr/hqk,qhd->khd/dot_general | solution.py:140
  590.3 5.5 all-to-all-start.4
  598.2 8.8 %fusion.73 = bf16[1536,3,64]{0,2,1:T(8,128)(2,1)S(1)} fusion(f32[1536,3,64]{0,2,1:T(8,128)} %fusion.125, bf16[512,3,64]{0,2,1:T(8,128)(2,1)S(1)} %bitcast.160, f32[3,512]{1,0:T(4,128)S(1)} %copy-done.62, f32[3,512,1536]{2,1,0:T(8,128)} %copy-done.6, pred[512,1536]{1,0:T(8,128)(4,1)S(1)} %copy-done.17), kind=kOutput, calls=%fused_computation.93 | convolution fusion | flops 319094784 | bytes 12195840 | tf_op jit(solution)/shard_map/while/body/eval_jaxpr/hqk,qhd->khd/dot_general | solution.py:140
  616.4 7.8 %all-to-all-done.4 = bf16[8,96,768]{2,1,0:T(8,128)(2,1)} async-done(((bf16[8,96,768]{2,1,0:T(8,128)(2,1)}), bf16[8,96,768]{2,1,0:T(8,128)(2,1)}, u32[]{:S(2)}, u32[]{:S(2)}) %all-to-all-start.4) | async-done | bytes 1179680 | tf_op jit(solution)/shard_map/all_to_all | solution.py:18
  685.7 19.5 %all-reduce.11.cloned.1.call-done = (bf16[1536,768]{1,0:T(8,128)(2,1)}, bf16[1536,768]{1,0:T(8,128)(2,1)}) async-done(((bf16[1536,768]{1,0:T(8,128)(2,1)}, bf16[1536,768]{1,0:T(8,128)(2,1)}), (bf16[1536,768]{1,0:T(8,128)(2,1)}, bf16[1536,768]{1,0:T(8,128)(2,1)})) %all-reduce.11.cloned.1.call-update) | async-done | bytes 4718608 | tf_op jit(solution)/shard_map/psum | solution.py:206
  711.7 5.5 all-to-all-start.7
  717.4 5.2 multiply_convert_fusion.4
  726.3 6.0 all-to-all-start.6
  732.9 5.9 all-to-all-done.6
  (267 shorter events, 167.5 us)
Async XLA Ops:
  8.0 77.0 %copy-start.1 = (bf16[1536,768]{1,0:T(8,128)(2,1)S(1)}, bf16[1536,768]{1,0:T(8,128)(2,1)}, u32[]{:S(2)}) copy-start(bf16[1536,768]{1,0:T(8,128)(2,1)} %param.27) | copy-start | bytes 7077892
  8.0 45.9 %copy-start.50 = (bf16[96,192]{1,0:T(8,128)(2,1)S(1)}, bf16[96,192]{1,0:T(8,128)(2,1)}, u32[]{:S(2)}) copy-start(bf16[96,192]{1,0:T(8,128)(2,1)} %param.30) | copy-start | bytes 110596
  8.0 304.2 %all-reduce.7.cloned.1.call-start = ((), (), s32[]{:S(2)}) async-start(), calls=%async_computation.8 | async-start | bytes 9437184 | tf_op jit(solution)/shard_map/psum | solution.py:199
  32.3 53.9 %copy-start.46 = (f32[768]{0:T(1024)}, f32[768]{0:T(1024)S(1)}, u32[]{:S(2)}) copy-start(f32[768]{0:T(1024)S(1)} %get-tuple-element.217) | copy-start | bytes 9220
  51.4 35.7 %copy-start.37 = (f32[1536]{0:T(1024)}, f32[1536]{0:T(1024)S(1)}, u32[]{:S(2)}) copy-start(f32[1536]{0:T(1024)S(1)} %broadcast_multiply_fusion.5) | copy-start | bytes 18436
  53.9 31.0 %copy-start.44 = (f32[1536]{0:T(1024)}, f32[1536]{0:T(1024)S(1)}, u32[]{:S(2)}) copy-start(f32[1536]{0:T(1024)S(1)} %add_rsqrt_fusion.1) | copy-start | bytes 18436
  86.2 36.1 %copy-start.3 = (bf16[1536,768]{1,0:T(8,128)(2,1)}, bf16[1536,768]{1,0:T(8,128)(2,1)S(1)}, u32[]{:S(2)}) copy-start(bf16[1536,768]{1,0:T(8,128)(2,1)S(1)} %fusion.17) | copy-start | bytes 7077892
  87.1 116.7 %copy-start.21 = (bf16[1536,192]{0,1:T(8,128)(2,1)}, bf16[1536,192]{0,1:T(8,128)(2,1)S(1)}, u32[]{:S(2)}) copy-start(bf16[1536,192]{0,1:T(8,128)(2,1)S(1)} %convolution_convert_fusion.2) | copy-start | bytes 1769476
  125.1 66.2 %copy-start.43 = (bf16[512,192]{0,1:T(8,128)(2,1)S(1)}, bf16[512,192]{0,1:T(8,128)(2,1)}, u32[]{:S(2)}) copy-start(bf16[512,192]{0,1:T(8,128)(2,1)} %slice.337) | copy-start | bytes 589828
  156.4 60.1 %copy-start.14 = (bf16[192,768]{0,1:T(8,128)(2,1)}, bf16[192,768]{0,1:T(8,128)(2,1)S(1)}, u32[]{:S(2)}) copy-start(bf16[192,768]{0,1:T(8,128)(2,1)S(1)} %all_gather.29) | copy-start | bytes 884740
  191.2 18.3 %copy-start.16 = (pred[512,1536]{1,0:T(8,128)(4,1)}, pred[512,1536]{1,0:T(8,128)(4,1)S(1)}, u32[]{:S(2)}) copy-start(pred[512,1536]{1,0:T(8,128)(4,1)S(1)} %fusion.50) | copy-start | bytes 2359300
  219.5 100.0 %all-gather.5.cloned.1.call-start = ((), (), s32[]{:S(2)}) async-start(), calls=%async_computation.9 | async-start | bytes 1327104 | tf_op jit(solution)/shard_map/all_gather | solution.py:166
  220.1 105.6 %all-gather.7.cloned.1.call-start = ((), (), s32[]{:S(2)}) async-start(), calls=%async_computation.10 | async-start | bytes 1327104 | tf_op jit(solution)/shard_map/all_gather | solution.py:167
  220.7 212.0 %all-reduce.9.cloned.1.call-start = ((), (), s32[]{:S(2)}) async-start(), calls=%async_computation.11 | async-start | bytes 9437184 | tf_op jit(solution)/shard_map/psum | solution.py:214
  347.9 242.4 %all-to-all-start.5 = ((bf16[8,768,96]{1,2,0:T(8,128)(2,1)}), bf16[8,768,96]{1,2,0:T(8,128)(2,1)}, u32[]{:S(2)}, u32[]{:S(2)}) async-start(bf16[8,768,96]{1,2,0:T(8,128)(2,1)} %bitcast.158), calls=%async_computation.5 | async-start | bytes 2359296 | tf_op jit(solution)/shard_map/all_to_all | solution.py:18
  470.0 22.3 %copy-start.36 = (f32[512,3,64]{0,2,1:T(8,128)S(1)}, f32[512,3,64]{0,2,1:T(8,128)}, u32[]{:S(2)}) copy-start(f32[512,3,64]{0,2,1:T(8,128)} %fusion.128) | copy-start | bytes 1179652
  503.2 26.8 %copy-start.63 = (f32[3,512]{1,0:T(4,128)S(1)}, f32[3,512]{1,0:T(4,128)}, u32[]{:S(2)}) copy-start(f32[3,512]{1,0:T(4,128)} %log_add_fusion.1) | copy-start | bytes 18436
  530.0 20.4 %copy-start.40 = (bf16[512,192]{0,1:T(8,128)(2,1)S(1)}, bf16[512,192]{0,1:T(8,128)(2,1)}, u32[]{:S(2)}) copy-start(bf16[512,192]{0,1:T(8,128)(2,1)} %copy-done.39) | copy-start | bytes 589828
  550.5 27.8 %copy-start.13 = (bf16[768,192]{1,0:T(8,128)(2,1)S(1)}, bf16[768,192]{1,0:T(8,128)(2,1)}, u32[]{:S(2)}) copy-start(bf16[768,192]{1,0:T(8,128)(2,1)} %copy-done.12) | copy-start | bytes 884740
  590.3 34.0 %all-to-all-start.4 = ((bf16[8,96,768]{2,1,0:T(8,128)(2,1)}), bf16[8,96,768]{2,1,0:T(8,128)(2,1)}, u32[]{:S(2)}, u32[]{:S(2)}) async-start(bf16[8,96,768]{2,1,0:T(8,128)(2,1)} %bitcast.157), calls=%async_computation.4 | async-start | bytes 2359296 | tf_op jit(solution)/shard_map/all_to_all | solution.py:18
  595.8 109.4 %all-reduce.11.cloned.1.call-start = ((), (), s32[]{:S(2)}) async-start(), calls=%async_computation.12 | async-start | bytes 9437184 | tf_op jit(solution)/shard_map/psum | solution.py:206
  624.3 15.5 %all-to-all-start.2 = ((bf16[8,96,192]{1,2,0:T(8,128)(2,1)}), bf16[8,96,192]{1,2,0:T(8,128)(2,1)S(1)}, u32[]{:S(2)}, u32[]{:S(2)}) async-start(bf16[8,96,192]{1,2,0:T(8,128)(2,1)} %copy.78), calls=%async_computation.2 | async-start | bytes 786432 | tf_op jit(solution)/shard_map/all_to_all | solution.py:18
  639.7 15.6 %all-to-all-start = ((bf16[8,96,192]{1,2,0:T(8,128)(2,1)}), bf16[8,96,192]{1,2,0:T(8,128)(2,1)}, u32[]{:S(2)}, u32[]{:S(2)}) async-start(bf16[8,96,192]{1,2,0:T(8,128)(2,1)} %copy.74), calls=%async_computation | async-start | bytes 786432 | tf_op jit(solution)/shard_map/all_to_all | solution.py:18
  655.3 14.8 %all-to-all-start.1 = ((bf16[8,96,192]{1,2,0:T(8,128)(2,1)}), bf16[8,96,192]{1,2,0:T(8,128)(2,1)}, u32[]{:S(2)}, u32[]{:S(2)}) async-start(bf16[8,96,192]{1,2,0:T(8,128)(2,1)} %copy.76), calls=%async_computation.1 | async-start | bytes 786432 | tf_op jit(solution)/shard_map/all_to_all | solution.py:18
  661.6 43.6 %copy-start.38 = (f32[1536]{0:T(1024)S(1)}, f32[1536]{0:T(1024)}, u32[]{:S(2)}) copy-start(f32[1536]{0:T(1024)} %copy-done.37) | copy-start | bytes 18436
  661.6 43.6 %copy-start.45 = (f32[1536]{0:T(1024)S(1)}, f32[1536]{0:T(1024)}, u32[]{:S(2)}) copy-start(f32[1536]{0:T(1024)} %copy-done.44) | copy-start | bytes 18436
  665.5 39.7 %copy-start.47 = (f32[768]{0:T(1024)S(1)}, f32[768]{0:T(1024)}, u32[]{:S(2)}) copy-start(f32[768]{0:T(1024)} %copy-done.46) | copy-start | bytes 9220
  670.1 14.8 %all-to-all-start.3 = ((bf16[8,192,96]{2,1,0:T(8,128)(2,1)}), bf16[8,192,96]{2,1,0:T(8,128)(2,1)S(1)}, u32[]{:S(2)}, u32[]{:S(2)}) async-start(bf16[8,192,96]{2,1,0:T(8,128)(2,1)} %bitcast.139), calls=%async_computation.3 | async-start | bytes 786432 | tf_op jit(solution)/shard_map/all_to_all | solution.py:18
  677.7 39.7 %copy-start.56 = (f32[1536]{0:T(1024)S(1)}, f32[1536]{0:T(1024)}, u32[]{:S(2)}) copy-start(f32[1536]{0:T(1024)} %fusion.154) | copy-start | bytes 18436
  705.2 17.4 %slice-start = ((s8[4718592]{0:T(1024)(128)(4,1)}), s8[524288]{0:T(1024)(128)(4,1)S(1)}, s32[]{:S(2)}) async-start(s8[4718592]{0:T(1024)(128)(4,1)} %bitcast.145), calls=%async_computation.13 | async-start | bytes 1048576
  711.7 14.6 %all-to-all-start.7 = ((bf16[8,2,96]{2,1,0:T(2,128)(2,1)}), bf16[8,2,96]{2,1,0:T(2,128)(2,1)S(1)}, u32[]{:S(2)}, u32[]{:S(2)}) async-start(bf16[8,2,96]{2,1,0:T(2,128)(2,1)} %copy.82), calls=%async_computation.7 | async-start | bytes 8192 | tf_op jit(solution)/shard_map/all_to_all | solution.py:18
  726.3 12.5 %all-to-all-start.6 = ((bf16[8,2,96]{2,1,0:T(2,128)(2,1)}), bf16[8,2,96]{2,1,0:T(2,128)(2,1)S(1)}, u32[]{:S(2)}, u32[]{:S(2)}) async-start(bf16[8,2,96]{2,1,0:T(2,128)(2,1)} %copy.81), calls=%async_computation.6 | async-start | bytes 8192 | tf_op jit(solution)/shard_map/all_to_all | solution.py:18
  (53 other events, 255.0 us)
Sparse Core Ops, SparseCore 0:
  219.7 92.5 all-reduce.6
  338.5 94.1 all-reduce.8
  610.3 94.8 all-reduce.10
Sparse Core Ops, SparseCore 1:
  222.2 39.9 all-gather.4
  264.2 40.0 all-gather.6
where the time goes:
time: 757 us; the launch traced here: 747 us
  matrix products  231 us (31%)
  waiting for transfers between devices  205 us (27%)
  blocking collectives  163 us (22%)
  other arithmetic  57.6 us (8%)
  starting transfers between devices  38.8 us (5%)
  local copies, waits for them, and re-layouts  34.2 us (5%)
  between operations  17.1 us (2%)
    psum x1, waiting for transfers between devices, per_device(): hidden = inputs + lax.psum(attn_partial, 'tensor')  90.3 us
    psum x1, waiting for transfers between devices, per_device(): grad_normed_two = lax.psum(mid_partial, 'tensor')  66.6 us
    dot_general x3, matrix products, attend_back(): jnp.einsum('hqk,qhd->khd', grad_raw, queries[begin_row:end_row], preferre...  57.9 us
    dot_general x3, matrix products, attend_back(): jnp.einsum('hqk,khd->qhd', grad_raw, key_rows[:end_row], preferred_elemen...  56.7 us
    all_to_all x8, starting transfers between devices, summed_on_arrival(): lax.all_to_all(cut_along(value, dim, length), axis, 0, 0, tiled=True)  38.4 us
    all_gather x1, blocking collectives, per_device(): lax.all_gather(w_out, 'batch', axis=1, tiled=True)  31.3 us
    all_gather x1, blocking collectives, per_device(): lax.all_gather(w_value, 'batch', axis=0, tiled=True)  31.2 us
    all_gather x1, blocking collectives, per_device(): lax.all_gather(w_query, 'batch', axis=0, tiled=True)  31.2 us
  transfers between devices with their start and end apart: 13, of which 9 were waited for; matrix products, arithmetic and copies ran while one was open for 34% of the time, Pallas kernels for 0%

commit v1 on v0

--- a/solution.py
+++ b/solution.py
@@ -196,7 +196,7 @@
     )
     mixed_low = mixed_heads.reshape(seq_rows, head_count * HD).astype(jnp.bfloat16)
     attn_partial = multiply(mixed_low, full_out)
-    hidden = inputs + lax.psum(attn_partial, "tensor")
+    hidden = inputs + jnp.sum(lax.all_gather(attn_partial, "tensor"), axis=0)
     normed_two, scaled_two, inverse_two = normalize_keep(hidden, gain_rows[1], shift_rows[1])
     normed_two_low = normed_two.astype(jnp.bfloat16)
     up_proj = multiply(normed_two_low, full_up)

time: 757 us -> 852 us (1.13)
  waiting for transfers between devices: 205 us -> 291 us
  other arithmetic: 57.6 us -> 68.3 us
    all_gather x0 -> x1, waiting for transfers between devices: none -> 116 us  [per_device(): hidden = inputs + jnp.sum(lax.all_gather(attn_partial, 'tensor'), axis=0)]
    psum x1 -> x0, waiting for transfers between devices: 90.3 us -> none  [per_device(): hidden = inputs + lax.psum(attn_partial, 'tensor')]
    all_gather x1, waiting for transfers between devices: 0.01 us -> 35.9 us  [per_device(): lax.all_gather(w_down, 'batch', axis=1, tiled=True)]
    all_gather x1, waiting for transfers between devices: 0.01 us -> 25.7 us  [per_device(): lax.all_gather(w_up, 'batch', axis=0, tiled=True)]
    reduce_sum x0 -> x1, other arithmetic: none -> 10.4 us  [per_device(): hidden = inputs + jnp.sum(lax.all_gather(attn_partial, 'tensor'), axis=0)]
  transfers between devices with their start and end apart: 13 -> 13, of which waited for: 9 -> 11; matrix products, arithmetic and copies ran while one was open for 34% -> 31% of each run, Pallas kernels for 0% -> 0%
where the time goes in v1:
time: 852 us; the launch traced here: 842 us
  waiting for transfers between devices  291 us (34%)
  matrix products  232 us (27%)
  blocking collectives  163 us (19%)
  other arithmetic  68.3 us (8%)
  starting transfers between devices  37.5 us (4%)
  local copies, waits for them, and re-layouts  34.2 us (4%)
  between operations  15.5 us (2%)
    all_gather x1, waiting for transfers between devices, per_device(): hidden = inputs + jnp.sum(lax.all_gather(attn_partial, 'tensor'), axis=0)  116 us
    psum x1, waiting for transfers between devices, per_device(): grad_normed_two = lax.psum(mid_partial, 'tensor')  65.9 us
    dot_general x3, matrix products, attend_back(): jnp.einsum('hqk,qhd->khd', grad_raw, queries[begin_row:end_row], preferre...  58.2 us
    dot_general x3, matrix products, attend_back(): jnp.einsum('hqk,khd->qhd', grad_raw, key_rows[:end_row], preferred_elemen...  56.3 us
    all_to_all x8, starting transfers between devices, summed_on_arrival(): lax.all_to_all(cut_along(value, dim, length), axis, 0, 0, tiled=True)  37 us
    all_gather x1, waiting for transfers between devices, per_device(): lax.all_gather(w_down, 'batch', axis=1, tiled=True)  35.9 us
    all_gather x1, blocking collectives, per_device(): lax.all_gather(w_out, 'batch', axis=1, tiled=True)  31.3 us
    all_gather x1, blocking collectives, per_device(): lax.all_gather(w_value, 'batch', axis=0, tiled=True)  31.2 us
  transfers between devices with their start and end apart: 13, of which 11 were waited for; matrix products, arithmetic and copies ran while one was open for 31% of the time, Pallas kernels for 0%

profile of v1, /device:TPU:0, one launch (start us, length us, event | category | flops | bytes accessed | tf_op | source)
XLA Modules:
  0.0 842.2 jit_solution(17484292192065140468)
XLA Ops:
  8.4 22.3 %all-gather.1 = bf16[8,96,2]{1,2,0:T(2,128)(2,1)S(1)} all-gather(bf16[1,96,2]{1,2,0:T(2,128)(2,1)} %bitcast.191), channel_id=1, replica_groups=mesh['batch'=8,'tensor'=4] {'batch'}, dimensions={0}, use_global_device_ids=true | all-gather | bytes 3456 | tf_op jit(solution)/shard_map/all_gather | solution.py:168
  31.4 16.4 %all-gather.2 = bf16[8,96,2]{1,2,0:T(2,128)(2,1)S(1)} all-gather(bf16[1,96,2]{1,2,0:T(2,128)(2,1)} %bitcast.192), channel_id=1, replica_groups=mesh['batch'=8,'tensor'=4] {'batch'}, dimensions={0}, use_global_device_ids=true | all-gather | bytes 3456 | tf_op jit(solution)/shard_map/all_gather | solution.py:169
  53.1 31.0 %all_gather.34 = bf16[768,192]{1,0:T(8,128)(2,1)S(1)} all-gather(bf16[96,192]{1,0:T(8,128)(2,1)S(1)} %copy-done.50), channel_id=1, replica_groups=mesh['batch'=8,'tensor'=4] {'batch'}, dimensions={0}, use_global_device_ids=true | all-gather | bytes 331776 | tf_op jit(solution)/shard_map/all_gather | solution.py:163
  87.8 31.2 %all_gather.32 = bf16[768,192]{1,0:T(8,128)(2,1)S(1)} all-gather(bf16[96,192]{1,0:T(8,128)(2,1)S(1)} %copy-done.51), channel_id=1, replica_groups=mesh['batch'=8,'tensor'=4] {'batch'}, dimensions={0}, use_global_device_ids=true | all-gather | bytes 331776 | tf_op jit(solution)/shard_map/all_gather | solution.py:164
  124.2 31.3 %all_gather.35 = bf16[192,768]{0,1:T(8,128)(2,1)S(1)} all-gather(bf16[192,96]{0,1:T(8,128)(2,1)} %copy.70), channel_id=1, replica_groups=mesh['batch'=8,'tensor'=4] {'batch'}, dimensions={1}, use_global_device_ids=true | all-gather | bytes 331776 | tf_op jit(solution)/shard_map/all_gather | solution.py:165
  155.6 31.2 %all_gather.33 = bf16[768,192]{1,0:T(8,128)(2,1)S(1)} all-gather(bf16[96,192]{1,0:T(8,128)(2,1)} %param.29), channel_id=1, replica_groups=mesh['batch'=8,'tensor'=4] {'batch'}, dimensions={0}, use_global_device_ids=true | all-gather | bytes 331776 | tf_op jit(solution)/shard_map/all_gather | solution.py:162
  209.5 6.4 fusion.150
  222.0 115.8 %all-gather.11.cloned.1.call-done = f32[6144,768]{1,0:T(8,128)} async-done(((f32[1536,768]{1,0:T(8,128)}), f32[6144,768]{1,0:T(8,128)}) %all-gather.11.cloned.1.call-update) | async-done | bytes 18874384 | tf_op jit(solution)/shard_map/all_gather | solution.py:199
  337.7 10.4 %reduce_sum.254 = f32[1536,768]{1,0:T(8,128)} reduce(f32[4,1536,768]{2,1,0:T(8,128)} %bitcast.150, f32[]{:T(128)} %constant.250.clone.1), dimensions={0}, to_apply=%region_8.9 | reduce | flops 3538944 | bytes 23592964 | tf_op jit(solution)/shard_map/reduce_sum | solution.py:199
  355.3 25.7 %all-gather.7.cloned.1.call-done = bf16[768,768]{1,0:T(8,128)(2,1)} async-done(((bf16[96,768]{1,0:T(8,128)(2,1)}), bf16[768,768]{1,0:T(8,128)(2,1)}) %all-gather.7.cloned.1.call-update) | async-done | bytes 1179664 | tf_op jit(solution)/shard_map/all_gather | solution.py:166
  381.0 6.1 fusion.203
  387.1 35.9 %all-gather.9.cloned.1.call-done = bf16[768,768]{0,1:T(8,128)(2,1)} async-done(((bf16[768,96]{0,1:T(8,128)(2,1)}), bf16[768,768]{0,1:T(8,128)(2,1)}) %all-gather.9.cloned.1.call-update) | async-done | bytes 1179664 | tf_op jit(solution)/shard_map/all_gather | solution.py:167
  423.1 7.0 fusion.31
  438.5 7.6 fusion.107
  450.6 5.5 convolution_convert_fusion.5
  456.2 6.7 convolution_convert_fusion
  462.9 65.9 %all-reduce.6.cloned.1.call-done = f32[1536,768]{1,0:T(8,128)} async-done(((f32[1536,768]{1,0:T(8,128)}), f32[1536,768]{1,0:T(8,128)}) %all-reduce.6.cloned.1.call-update) | async-done | bytes 4718608 | tf_op jit(solution)/shard_map/psum | solution.py:214
  528.8 5.6 multiply_reduce_fusion.2
  546.7 9.8 %fusion.128 = f32[512,3,64]{0,2,1:T(8,128)} fusion(bf16[512,3,64]{0,2,1:T(8,128)(2,1)} %bitcast.180, f32[3,512,512]{1,2,0:T(8,128)} %fusion.205, f32[3,512,512]{1,2,0:T(8,128)} %copy-done.18, f32[3,512]{1,0:T(4,128)S(1)} %copy-done.61, pred[512,512]{0,1:T(8,128)(4,1)} %copy-done.28), kind=kOutput, calls=%fused_computation.130 | convolution fusion | flops 114821120 | bytes 7149568 | tf_op jit(solution)/shard_map/while/body/eval_jaxpr/hqk,qhd->khd/dot_general | solution.py:132
  566.4 20.1 %fusion.145 = bf16[3,64,512]{2,1,0:T(8,128)(2,1)} fusion(bf16[1024,3,64]{0,2,1:T(8,128)(2,1)} %bitcast.173, f32[3,512,1024]{2,1,0:T(8,128)} %fusion.206, f32[3,512,1024]{2,1,0:T(8,128)} %copy-done.7, f32[3,512]{1,0:T(4,128)} %log_add_fusion.1, pred[512,1024]{1,0:T(8,128)(4,1)} %copy-done.23), kind=kOutput, calls=%fused_computation.139 | convolution fusion | flops 229739008 | bytes 13703168 | tf_op jit(solution)/shard_map/while/body/eval_jaxpr/hqk,khd->qhd/dot_general | solution.py:127
  589.8 9.8 %fusion.141 = bf16[3,64,512]{2,1,0:T(8,128)(2,1)} fusion(bf16[512,3,64]{0,2,1:T(8,128)(2,1)} %bitcast.181, f32[3,512,512]{1,2,0:T(8,128)} %fusion.205, f32[3,512,512]{1,2,0:T(8,128)} %copy-done.18, f32[3,512]{1,0:T(4,128)S(1)} %copy-done.61, pred[512,512]{0,1:T(8,128)(4,1)} %copy-done.28), kind=kOutput, calls=%fused_computation.137 | convolution fusion | flops 114919424 | bytes 6952960 | tf_op jit(solution)/shard_map/while/body/eval_jaxpr/hqk,khd->qhd/dot_general | solution.py:127
  599.6 26.4 %fusion.138 = bf16[3,64,512]{2,1,0:T(8,128)(2,1)} fusion(bf16[1536,3,64]{0,2,1:T(8,128)(2,1)S(1)} %bitcast.156, f32[3,512,1536]{2,1,0:T(8,128)} %fusion.207, f32[3,512,1536]{2,1,0:T(8,128)} %copy-done.6, f32[3,512]{1,0:T(4,128)S(1)} %copy-done.62, pred[512,1536]{1,0:T(8,128)(4,1)} %copy-done.16), kind=kOutput, calls=%fused_computation.136 | convolution fusion | flops 344558592 | bytes 20453376 | tf_op jit(solution)/shard_map/while/body/eval_jaxpr/hqk,khd->qhd/dot_general | solution.py:127
  626.0 20.5 %fusion.119 = f32[1536,3,64]{0,2,1:T(8,128)} fusion(f32[1536,3,64]{0,2,1:T(8,128)} %scatter-add.14, bf16[512,3,64]{0,2,1:T(8,128)(2,1)} %bitcast.178, f32[3,512,1024]{2,1,0:T(8,128)} %fusion.206, f32[3,512,1024]{2,1,0:T(8,128)} %copy-done.7, f32[3,512]{1,0:T(4,128)S(1)} %copy-done.63, pred[512,1024]{1,0:T(8,128)(4,1)} %copy-done.23), kind=kOutput, calls=%fused_computation.123 | convolution fusion | flops 229837312 | bytes 28000256 | tf_op jit(solution)/shard_map/while/body/eval_jaxpr/hqk,qhd->khd/dot_general | solution.py:132
  646.5 27.9 %fusion.76 = bf16[1536,3,64]{0,2,1:T(8,128)(2,1)} fusion(f32[1536,3,64]{0,2,1:T(8,128)} %fusion.119, bf16[512,3,64]{0,2,1:T(8,128)(2,1)S(1)} %bitcast.176, f32[3,512,1536]{2,1,0:T(8,128)} %fusion.207, f32[3,512,1536]{2,1,0:T(8,128)} %copy-done.6, f32[3,512]{1,0:T(4,128)S(1)} %copy-done.62, pred[512,1536]{1,0:T(8,128)(4,1)} %copy-done.16), kind=kOutput, calls=%fused_computation.94 | convolution fusion | flops 345050112 | bytes 21633024 | tf_op jit(solution)/shard_map/while/body/eval_jaxpr/hqk,qhd->khd/dot_general | solution.py:132
  678.5 7.9 fusion.125
  686.4 5.5 all-to-all-start.4
  694.3 8.8 %fusion.73 = bf16[1536,3,64]{0,2,1:T(8,128)(2,1)S(1)} fusion(f32[1536,3,64]{0,2,1:T(8,128)} %fusion.125, bf16[512,3,64]{0,2,1:T(8,128)(2,1)S(1)} %bitcast.162, f32[3,512]{1,0:T(4,128)S(1)} %copy-done.62, f32[3,512,1536]{2,1,0:T(8,128)} %copy-done.6, pred[512,1536]{1,0:T(8,128)(4,1)S(1)} %copy-done.17), kind=kOutput, calls=%fused_computation.93 | convolution fusion | flops 319094784 | bytes 12195840 | tf_op jit(solution)/shard_map/while/body/eval_jaxpr/hqk,qhd->khd/dot_general | solution.py:140
  712.5 7.9 all-to-all-done.4
  781.8 19.4 %all-reduce.8.cloned.1.call-done = (bf16[1536,768]{1,0:T(8,128)(2,1)}, bf16[1536,768]{1,0:T(8,128)(2,1)}) async-done(((bf16[1536,768]{1,0:T(8,128)(2,1)}, bf16[1536,768]{1,0:T(8,128)(2,1)}), (bf16[1536,768]{1,0:T(8,128)(2,1)}, bf16[1536,768]{1,0:T(8,128)(2,1)})) %all-reduce.8.cloned.1.call-update) | async-done | bytes 4718608 | tf_op jit(solution)/shard_map/psum | solution.py:206
  807.8 5.5 all-to-all-start.7
  822.4 6.0 all-to-all-start.6
  829.0 5.9 all-to-all-done.6
  (268 shorter events, 183.1 us)
Async XLA Ops:
  7.2 77.0 %copy-start.1 = (bf16[1536,768]{1,0:T(8,128)(2,1)S(1)}, bf16[1536,768]{1,0:T(8,128)(2,1)}, u32[]{:S(2)}) copy-start(bf16[1536,768]{1,0:T(8,128)(2,1)} %param.27) | copy-start | bytes 7077892
  7.2 45.9 %copy-start.50 = (bf16[96,192]{1,0:T(8,128)(2,1)S(1)}, bf16[96,192]{1,0:T(8,128)(2,1)}, u32[]{:S(2)}) copy-start(bf16[96,192]{1,0:T(8,128)(2,1)} %param.30) | copy-start | bytes 110596
  7.2 330.5 %all-gather.11.cloned.1.call-start = ((), (), s32[]{:S(2)}) async-start(), calls=%async_computation.11 | async-start | bytes 23592960 | tf_op jit(solution)/shard_map/all_gather | solution.py:199
  31.4 53.9 %copy-start.46 = (f32[768]{0:T(1024)}, f32[768]{0:T(1024)S(1)}, u32[]{:S(2)}) copy-start(f32[768]{0:T(1024)S(1)} %get-tuple-element.217) | copy-start | bytes 9220
  50.6 35.7 %copy-start.37 = (f32[1536]{0:T(1024)}, f32[1536]{0:T(1024)S(1)}, u32[]{:S(2)}) copy-start(f32[1536]{0:T(1024)S(1)} %broadcast_multiply_fusion.5) | copy-start | bytes 18436
  53.1 31.0 %copy-start.44 = (f32[1536]{0:T(1024)}, f32[1536]{0:T(1024)S(1)}, u32[]{:S(2)}) copy-start(f32[1536]{0:T(1024)S(1)} %add_rsqrt_fusion.1) | copy-start | bytes 18436
  85.3 36.1 %copy-start.3 = (bf16[1536,768]{1,0:T(8,128)(2,1)}, bf16[1536,768]{1,0:T(8,128)(2,1)S(1)}, u32[]{:S(2)}) copy-start(bf16[1536,768]{1,0:T(8,128)(2,1)S(1)} %fusion.17) | copy-start | bytes 7077892
  86.3 117.0 %copy-start.21 = (bf16[1536,192]{0,1:T(8,128)(2,1)}, bf16[1536,192]{0,1:T(8,128)(2,1)S(1)}, u32[]{:S(2)}) copy-start(bf16[1536,192]{0,1:T(8,128)(2,1)S(1)} %convolution_convert_fusion.2) | copy-start | bytes 1769476
  124.2 66.2 %copy-start.43 = (bf16[512,192]{0,1:T(8,128)(2,1)S(1)}, bf16[512,192]{0,1:T(8,128)(2,1)}, u32[]{:S(2)}) copy-start(bf16[512,192]{0,1:T(8,128)(2,1)} %slice.337) | copy-start | bytes 589828
  155.5 60.5 %copy-start.14 = (bf16[192,768]{0,1:T(8,128)(2,1)}, bf16[192,768]{0,1:T(8,128)(2,1)S(1)}, u32[]{:S(2)}) copy-start(bf16[192,768]{0,1:T(8,128)(2,1)S(1)} %all_gather.35) | copy-start | bytes 884740
  190.4 18.6 %copy-start.16 = (pred[512,1536]{1,0:T(8,128)(4,1)}, pred[512,1536]{1,0:T(8,128)(4,1)S(1)}, u32[]{:S(2)}) copy-start(pred[512,1536]{1,0:T(8,128)(4,1)S(1)} %fusion.50) | copy-start | bytes 2359300
  219.1 162.0 %all-gather.7.cloned.1.call-start = ((), (), s32[]{:S(2)}) async-start(), calls=%async_computation.8 | async-start | bytes 1327104 | tf_op jit(solution)/shard_map/all_gather | solution.py:166
  219.8 203.3 %all-gather.9.cloned.1.call-start = ((), (), s32[]{:S(2)}) async-start(), calls=%async_computation.9 | async-start | bytes 1327104 | tf_op jit(solution)/shard_map/all_gather | solution.py:167
  220.6 308.2 %all-reduce.6.cloned.1.call-start = ((), (), s32[]{:S(2)}) async-start(), calls=%async_computation.10 | async-start | bytes 9437184 | tf_op jit(solution)/shard_map/psum | solution.py:214
  446.1 240.2 %all-to-all-start.5 = ((bf16[8,768,96]{1,2,0:T(8,128)(2,1)}), bf16[8,768,96]{1,2,0:T(8,128)(2,1)}, u32[]{:S(2)}, u32[]{:S(2)}) async-start(bf16[8,768,96]{1,2,0:T(8,128)(2,1)} %bitcast.160), calls=%async_computation.5 | async-start | bytes 2359296 | tf_op jit(solution)/shard_map/all_to_all | solution.py:18
  566.4 22.2 %copy-start.36 = (f32[512,3,64]{0,2,1:T(8,128)S(1)}, f32[512,3,64]{0,2,1:T(8,128)}, u32[]{:S(2)}) copy-start(f32[512,3,64]{0,2,1:T(8,128)} %fusion.128) | copy-start | bytes 1179652
  599.5 26.4 %copy-start.63 = (f32[3,512]{1,0:T(4,128)S(1)}, f32[3,512]{1,0:T(4,128)}, u32[]{:S(2)}) copy-start(f32[3,512]{1,0:T(4,128)} %log_add_fusion.1) | copy-start | bytes 18436
  626.0 20.5 %copy-start.40 = (bf16[512,192]{0,1:T(8,128)(2,1)S(1)}, bf16[512,192]{0,1:T(8,128)(2,1)}, u32[]{:S(2)}) copy-start(bf16[512,192]{0,1:T(8,128)(2,1)} %copy-done.39) | copy-start | bytes 589828
  646.5 27.9 %copy-start.13 = (bf16[768,192]{1,0:T(8,128)(2,1)S(1)}, bf16[768,192]{1,0:T(8,128)(2,1)}, u32[]{:S(2)}) copy-start(bf16[768,192]{1,0:T(8,128)(2,1)} %copy-done.12) | copy-start | bytes 884740
  686.4 34.0 %all-to-all-start.4 = ((bf16[8,96,768]{2,1,0:T(8,128)(2,1)}), bf16[8,96,768]{2,1,0:T(8,128)(2,1)}, u32[]{:S(2)}, u32[]{:S(2)}) async-start(bf16[8,96,768]{2,1,0:T(8,128)(2,1)} %bitcast.159), calls=%async_computation.4 | async-start | bytes 2359296 | tf_op jit(solution)/shard_map/all_to_all | solution.py:18
  691.9 109.3 %all-reduce.8.cloned.1.call-start = ((), (), s32[]{:S(2)}) async-start(), calls=%async_computation.12 | async-start | bytes 9437184 | tf_op jit(solution)/shard_map/psum | solution.py:206
  720.4 15.5 %all-to-all-start.2 = ((bf16[8,96,192]{1,2,0:T(8,128)(2,1)}), bf16[8,96,192]{1,2,0:T(8,128)(2,1)S(1)}, u32[]{:S(2)}, u32[]{:S(2)}) async-start(bf16[8,96,192]{1,2,0:T(8,128)(2,1)} %copy.78), calls=%async_computation.2 | async-start | bytes 786432 | tf_op jit(solution)/shard_map/all_to_all | solution.py:18
  735.9 15.6 %all-to-all-start = ((bf16[8,96,192]{1,2,0:T(8,128)(2,1)}), bf16[8,96,192]{1,2,0:T(8,128)(2,1)}, u32[]{:S(2)}, u32[]{:S(2)}) async-start(bf16[8,96,192]{1,2,0:T(8,128)(2,1)} %copy.74), calls=%async_computation | async-start | bytes 786432 | tf_op jit(solution)/shard_map/all_to_all | solution.py:18
  751.4 14.9 %all-to-all-start.1 = ((bf16[8,96,192]{1,2,0:T(8,128)(2,1)}), bf16[8,96,192]{1,2,0:T(8,128)(2,1)}, u32[]{:S(2)}, u32[]{:S(2)}) async-start(bf16[8,96,192]{1,2,0:T(8,128)(2,1)} %copy.76), calls=%async_computation.1 | async-start | bytes 786432 | tf_op jit(solution)/shard_map/all_to_all | solution.py:18
  757.7 43.5 %copy-start.38 = (f32[1536]{0:T(1024)S(1)}, f32[1536]{0:T(1024)}, u32[]{:S(2)}) copy-start(f32[1536]{0:T(1024)} %copy-done.37) | copy-start | bytes 18436
  757.7 43.5 %copy-start.45 = (f32[1536]{0:T(1024)S(1)}, f32[1536]{0:T(1024)}, u32[]{:S(2)}) copy-start(f32[1536]{0:T(1024)} %copy-done.44) | copy-start | bytes 18436
  761.6 39.6 %copy-start.47 = (f32[768]{0:T(1024)S(1)}, f32[768]{0:T(1024)}, u32[]{:S(2)}) copy-start(f32[768]{0:T(1024)} %copy-done.46) | copy-start | bytes 9220
  766.3 14.8 %all-to-all-start.3 = ((bf16[8,192,96]{2,1,0:T(8,128)(2,1)}), bf16[8,192,96]{2,1,0:T(8,128)(2,1)S(1)}, u32[]{:S(2)}, u32[]{:S(2)}) async-start(bf16[8,192,96]{2,1,0:T(8,128)(2,1)} %bitcast.140), calls=%async_computation.3 | async-start | bytes 786432 | tf_op jit(solution)/shard_map/all_to_all | solution.py:18
  773.8 39.6 %copy-start.56 = (f32[1536]{0:T(1024)S(1)}, f32[1536]{0:T(1024)}, u32[]{:S(2)}) copy-start(f32[1536]{0:T(1024)} %fusion.154) | copy-start | bytes 18436
  801.2 17.4 %slice-start = ((s8[4718592]{0:T(1024)(128)(4,1)}), s8[524288]{0:T(1024)(128)(4,1)S(1)}, s32[]{:S(2)}) async-start(s8[4718592]{0:T(1024)(128)(4,1)} %bitcast.146), calls=%async_computation.13 | async-start | bytes 1048576
  807.8 14.6 %all-to-all-start.7 = ((bf16[8,2,96]{2,1,0:T(2,128)(2,1)}), bf16[8,2,96]{2,1,0:T(2,128)(2,1)S(1)}, u32[]{:S(2)}, u32[]{:S(2)}) async-start(bf16[8,2,96]{2,1,0:T(2,128)(2,1)} %copy.82), calls=%async_computation.7 | async-start | bytes 8192 | tf_op jit(solution)/shard_map/all_to_all | solution.py:18
  822.4 12.5 %all-to-all-start.6 = ((bf16[8,2,96]{2,1,0:T(2,128)(2,1)}), bf16[8,2,96]{2,1,0:T(2,128)(2,1)S(1)}, u32[]{:S(2)}, u32[]{:S(2)}) async-start(bf16[8,2,96]{2,1,0:T(2,128)(2,1)} %copy.81), calls=%async_computation.6 | async-start | bytes 8192 | tf_op jit(solution)/shard_map/all_to_all | solution.py:18
  (53 other events, 256.7 us)
Sparse Core Ops, SparseCore 0:
  219.2 118.5 all-gather.10
  339.9 41.0 all-gather.6
  383.2 39.8 all-gather.8
  436.0 92.7 all-reduce.5
  706.4 94.8 all-reduce.7
